TPU v7x, 32 devices: a whole 2x2x4 slice. The times are simulated.
32 devices in a mesh: loan: 8 (over y, x, core), path: 4 (over z).
Axes of the slice: x: 2, y: 2, z: 4, core: 2. Of those that a mesh axis runs over, the one named last changes fastest.
Arguments:
- price_moves: bfloat16 [12, 416, 512], P(None, 'loan', 'path'), may hold values from -0.1796875 to 0.1796875
- block_regions: int32 [16, 32], P('loan'), may hold values from 0 to 415
- region_slot: int32 [4096], P('loan'), may hold values from 0 to 31
- block_pools: int32 [16, 32], P('loan'), may hold values from 0 to 511, as said below
- pool_slot: int32 [4096], P('loan'), may hold values from 0 to 31, as said below
- init_state: int32 [4096], P('loan'), may hold values from 0 to 5
- balance: float32 [4096], P('loan'), may hold values from 0.5 to 2
- loan_to_value: float32 [4096], P('loan'), may hold values from 0.5 to 1.3
- hazard_base: float32 [2, 6], replicated, may hold values from -4 to -1
- hazard_slope: float32 [2, 6], replicated, may hold values from 1 to 4
- attach_bps: int32 [512, 6], P('loan'), may hold values from 0 to 2995, as said below
Outputs:
- expected_loss: float32 [6, 3, 512], P(None, None, 'loan')
- path_loss: float32 [6, 512, 512], P(None, 'loan', 'path')
Inputs may be any that keep to these rules, and one draw needn't show every extreme that they name: `block_pools`: over all blocks' lists every pool appears exactly once. The lists of the blocks held by one index of loan name exactly 64 // 8 pools of every owner, owner k being the index of loan that holds pools k * 64 to (k + 1) * 64 - 1. `pool_slot`: every aligned block of 256 loans uses each position of its pool list at least once. `attach_bps`: each row starts at 0 and rises by 100 to 599 from one tranche to the next.
All inputs are finite; a program needn't handle non-finite values.
Results may differ from a plain program's by a relative error of at most 0.0003.
Values may be sent and summed in bfloat16 or wider, within the bound.
No kernel may reach another device: no remote copies, remote signals or barrier semaphores. Data moves between devices by JAX's collectives and lax.ppermute only.
A program may use at most 64 MiB of HBM per device.

v0:
```python
import jax
import jax.numpy as jnp
from jax import lax
from jax.sharding import PartitionSpec as P

BLOCK = 256
stress_scale = 0.3


def roll_months(
    routed, path_place, path_count, log_value, initial, balance, hazard_base, hazard_slope
):
    months = routed.shape[0]
    month_place = (jnp.arange(months, dtype=jnp.float32) + 1.0) / months
    stress_path = (
        stress_scale * ((path_place + 0.5) / path_count)[None, :, None] * month_place[:, None, None]
    )
    cumulated = jnp.cumsum(routed, axis=0) - stress_path
    level = log_value[None, None, :] - cumulated
    start_state = jnp.broadcast_to(
        initial[:, None, :], (initial.shape[0], routed.shape[1], routed.shape[2])
    )
    loss_start = jnp.zeros(routed.shape[1:], jnp.float32)

    def month_step(state_pair, ltv_now):
        state, loss_sum = state_pair
        roll_rate = jax.nn.sigmoid(
            hazard_base[0][:, None, None] + hazard_slope[0][:, None, None] * ltv_now[None]
        )
        cure_rate = jax.nn.sigmoid(
            hazard_base[1][:, None, None] - hazard_slope[1][:, None, None] * ltv_now[None]
        )
        stay_rate = (1.0 - roll_rate) * (1.0 - cure_rate)
        forward = state * roll_rate
        backward = state * (1.0 - roll_rate) * cure_rate
        first_state = state[0] * stay_rate[0] + jnp.sum(backward[1:], axis=0)
        rest_state = forward[:-1] + state[1:] * stay_rate[1:]
        updated = jnp.concatenate([first_state[None], rest_state], axis=0)
        severity = 0.1 + 0.5 * jax.nn.sigmoid(3.0 * ltv_now)
        loss_next = loss_sum + balance[None, :] * severity * forward[-1]
        return ((updated, loss_next), loss_next)

    state_pair, history = lax.scan(month_step, (start_state, loss_start), level)
    return history[3::4]


def lookup(lookup_table, positions):
    matches = positions[:, None] == jnp.arange(lookup_table.shape[0], dtype=jnp.int32)[None, :]
    return jnp.sum(jnp.where(matches, lookup_table[None, :], 0), axis=1)


def shards(
    price_moves,
    block_regions,
    region_slot,
    block_pools,
    pool_slot,
    init_state,
    balance,
    loan_to_value,
    hazard_base,
    hazard_slope,
    attach_bps,
):
    loan_dev = region_slot.shape[0]
    months, metro_dev, path_dev = price_moves.shape
    pool_dev = attach_bps.shape[0]
    dates = months // 4
    block_index = jnp.arange(loan_dev, dtype=jnp.int32) // BLOCK
    metro_id = lookup(block_regions.reshape(-1), block_index * block_regions.shape[1] + region_slot)
    slot_id = block_index * block_pools.shape[1] + pool_slot
    listed_pools = block_pools.reshape(-1)
    shard = lax.all_gather(price_moves, "loan", axis=1, tiled=True)
    chooser = (metro_id[None, :] == jnp.arange(shard.shape[1], dtype=jnp.int32)[:, None]).astype(
        jnp.bfloat16
    )
    routed = jnp.einsum("mrp,rl->mpl", shard, chooser, preferred_element_type=jnp.float32)
    path_count = path_dev * lax.axis_size("path")
    path_place = (lax.axis_index("path") * path_dev + jnp.arange(path_dev, dtype=jnp.int32)).astype(
        jnp.float32
    )
    initial = (
        init_state[None, :] == jnp.arange(hazard_base.shape[1], dtype=jnp.int32)[:, None]
    ).astype(jnp.float32)
    losses = roll_months(
        routed,
        path_place,
        float(path_count),
        jnp.log(loan_to_value),
        initial,
        balance,
        hazard_base,
        hazard_slope,
    )
    loss_rows = losses.reshape(dates * path_dev, loan_dev)
    contract = (((1,), (1,)), ((), ()))
    slot_count = listed_pools.shape[0]
    members = (slot_id[None, :] == jnp.arange(slot_count, dtype=jnp.int32)[:, None]).astype(
        jnp.float32
    )
    slot_loss = lax.dot_general(
        members,
        loss_rows,
        contract,
        precision=lax.Precision.HIGHEST,
        preferred_element_type=jnp.float32,
    )
    slot_balance = jnp.dot(
        members, balance, precision=lax.Precision.HIGHEST, preferred_element_type=jnp.float32
    )
    ranking = jnp.argsort(listed_pools // pool_dev, stable=True)
    outgoing = (
        slot_loss[ranking],
        slot_balance[ranking],
        listed_pools[ranking].astype(jnp.float32),
    )
    got_loss, got_balance, got_pool = (
        lax.all_to_all(outgoing[0], "loan", split_axis=0, concat_axis=0, tiled=True),
        lax.all_to_all(outgoing[1], "loan", split_axis=0, concat_axis=0, tiled=True),
        lax.all_to_all(outgoing[2], "loan", split_axis=0, concat_axis=0, tiled=True),
    )
    local_pool = got_pool - (lax.axis_index("loan") * pool_dev).astype(jnp.float32)
    placing = (
        local_pool[None, :] == jnp.arange(pool_dev, dtype=jnp.int32)[:, None].astype(jnp.float32)
    ).astype(jnp.float32)
    pool_loss = jnp.dot(
        placing, got_loss, precision=lax.Precision.HIGHEST, preferred_element_type=jnp.float32
    )
    notional = jnp.dot(
        placing, got_balance, precision=lax.Precision.HIGHEST, preferred_element_type=jnp.float32
    )
    attach = attach_bps.astype(jnp.float32) / 10000.0
    detach = jnp.concatenate([attach[:, 1:], jnp.ones((pool_dev, 1), jnp.float32)], axis=1)
    ratio = pool_loss.reshape(pool_dev, dates, path_dev) / notional[:, None, None]
    lower = attach.T[:, :, None, None]
    height = (detach - attach).T[:, :, None, None]
    shares = jnp.clip((ratio[None] - lower) / height, 0.0, 1.0)
    partial_value = jnp.sum(shares, axis=3).transpose(0, 2, 1)
    expected_loss = lax.psum(partial_value, "path") / path_count
    return (expected_loss, shares[:, :, -1, :])


def solution(mesh):
    in_specs = (
        P(None, "loan", "path"),
        P("loan", None),
        P("loan"),
        P("loan", None),
        P("loan"),
        P("loan"),
        P("loan"),
        P("loan"),
        P(),
        P(),
        P("loan", None),
    )
    out_specs = (P(None, None, "loan"), P(None, "loan", "path"))
    return jax.shard_map(shards, mesh=mesh, in_specs=in_specs, out_specs=out_specs, check_vma=False)
```

profile of v0, /device:TPU:0, one launch (start us, length us, event | category | flops | bytes accessed | tf_op | source)
XLA Modules:
  0.0 173.0 jit_solution(12231268295599842908)
XLA Ops:
  13.2 5.2 %all-to-all-start = ((f32[8,8,1]{1,2,0:T(1,128)}), f32[8,8,1]{1,2,0:T(1,128)S(1)}, u32[]{:S(2)}, u32[]{:S(2)}) async-start(f32[8,8,1]{1,2,0:T(1,128)} %bitcast), calls=%async_computation | async-start | bytes 8192 | tf_op jit(solution)/shard_map/all_to_all | solution.py:120
  23.0 3.3 %all-to-all-start.2 = ((f32[8,8,1]{1,2,0:T(1,128)}), f32[8,8,1]{1,2,0:T(1,128)S(1)}, u32[]{:S(2)}, u32[]{:S(2)}) async-start(f32[8,8,1]{1,2,0:T(1,128)} %bitcast.10), calls=%async_computation.2 | async-start | bytes 8192 | tf_op jit(solution)/shard_map/all_to_all | solution.py:119
  26.5 4.4 %all-to-all-done.2 = f32[8,8,1]{1,2,0:T(1,128)S(1)} async-done(((f32[8,8,1]{1,2,0:T(1,128)}), f32[8,8,1]{1,2,0:T(1,128)S(1)}, u32[]{:S(2)}, u32[]{:S(2)}) %all-to-all-start.2) | async-done | bytes 288 | tf_op jit(solution)/shard_map/all_to_all | solution.py:119
  32.2 6.6 %all-gather.2.cloned.1.call-done = bf16[12,416,128]{2,0,1:T(8,128)(2,1)} async-done(((bf16[12,52,128]{2,0,1:T(8,128)(2,1)}), bf16[12,416,128]{2,0,1:T(8,128)(2,1)}) %all-gather.2.cloned.1.call-update) | async-done | bytes 1277968 | tf_op jit(solution)/shard_map/all_gather | solution.py:73
  38.8 2.5 %fusion.9 = f32[512,12,128]{2,0,1:T(8,128)S(1)} fusion(bf16[12,416,128]{2,0,1:T(8,128)(2,1)} %all-gather.2.cloned.1.call-done, s32[512]{0:T(512)S(1)} %select_reduce_fusion), kind=kOutput, calls=%fused_computation.28 | convolution fusion | flops 654524416 | bytes 4425728 | tf_op jit(solution)/shard_map/mrp,rl->mpl/dot_general | solution.py:77
  44.1 89.9 %while.15 = (s32[]{:T(128)}, f32[6,128,512]{2,1,0:T(8,128)S(1)}, f32[128,512]{1,0:T(8,128)}, f32[12,128,512]{2,1,0:T(8,128)}, f32[2,6]{1,0:T(2,128)S(1)}, /*inde...) while((s32[]{:T(128)}, f32[6,128,512]{2,1,0:T(8,128)S(1)}, ...), condition=%wide.region_5.6_spmd.clone, body=%wide.region_3.5_spmd.clone.sunk | while | flops 8257539 | bytes 34343880 | solution.py:43
  46.4 2.7 %fusion.43 = (f32[128,512]{1,0:T(8,128)}, f32[5,128,512]{2,1,0:T(8,128)}) fusion(f32[6,128,512]{2,1,0:T(8,128)S(1)} %get-tuple-element.209, f32[6,128,512]{2,1,0:T(8,128)S(1)} %get-tuple-element.210, f32[6,128,512]{2,1,0:T(8,128)S(1)} %get-tuple-element.229, f32[6,128,512]{2,1,0:T(8,128)S(1)} %get-tuple-element.211, ...), kind=kLoop, calls=%fused_computation.10.clone.1 | loop fusion | flops 1572864 | bytes 8126464 | tf_op jit(solution)/shard_map/while/body/eval_jaxpr/reduce_sum | solution.py:36
  53.9 2.7 %fusion.43 = (f32[128,512]{1,0:T(8,128)}, f32[5,128,512]{2,1,0:T(8,128)}) fusion(f32[6,128,512]{2,1,0:T(8,128)S(1)} %get-tuple-element.209, f32[6,128,512]{2,1,0:T(8,128)S(1)} %get-tuple-element.210, f32[6,128,512]{2,1,0:T(8,128)S(1)} %get-tuple-element.229, f32[6,128,512]{2,1,0:T(8,128)S(1)} %get-tuple-element.211, ...), kind=kLoop, calls=%fused_computation.10.clone.1 | loop fusion | flops 1572864 | bytes 8126464 | tf_op jit(solution)/shard_map/while/body/eval_jaxpr/reduce_sum | solution.py:36
  56.6 2.2 %bitcast_dynamic-update-slice_fusion.2 = (f32[12,128,512]{2,1,0:T(8,128)}, f32[128,512]{1,0:T(8,128)}, f32[1,128,512]{2,1,0:T(8,128)S(1)}) fusion(f32[12,128,512]{2,1,0:T(8,128)} %get-tuple-element.231, s32[]{:T(128)} %get-tuple-element.228, f32[6,128,512]{2,1,0:T(8,128)S(1)} %get-tuple-element.212, f32[1,128,512]{2,1,0:T(8,128)S(1)} %copy.39, ...), kind=kLoop, calls=%fused_computation.19.clone.1 | loop fusion | flops 786432 | bytes 2361857 | tf_op jit(solution)/shard_map/while/body/jit(dynamic_update_index_in_dim)/dynamic_update_slice | solution.py:43
  61.4 2.7 %fusion.43 = (f32[128,512]{1,0:T(8,128)}, f32[5,128,512]{2,1,0:T(8,128)}) fusion(f32[6,128,512]{2,1,0:T(8,128)S(1)} %get-tuple-element.209, f32[6,128,512]{2,1,0:T(8,128)S(1)} %get-tuple-element.210, f32[6,128,512]{2,1,0:T(8,128)S(1)} %get-tuple-element.229, f32[6,128,512]{2,1,0:T(8,128)S(1)} %get-tuple-element.211, ...), kind=kLoop, calls=%fused_computation.10.clone.1 | loop fusion | flops 1572864 | bytes 8126464 | tf_op jit(solution)/shard_map/while/body/eval_jaxpr/reduce_sum | solution.py:36
  64.1 2.2 %bitcast_dynamic-update-slice_fusion.2 = (f32[12,128,512]{2,1,0:T(8,128)}, f32[128,512]{1,0:T(8,128)}, f32[1,128,512]{2,1,0:T(8,128)S(1)}) fusion(f32[12,128,512]{2,1,0:T(8,128)} %get-tuple-element.231, s32[]{:T(128)} %get-tuple-element.228, f32[6,128,512]{2,1,0:T(8,128)S(1)} %get-tuple-element.212, f32[1,128,512]{2,1,0:T(8,128)S(1)} %copy.39, ...), kind=kLoop, calls=%fused_computation.19.clone.1 | loop fusion | flops 786432 | bytes 2361857 | tf_op jit(solution)/shard_map/while/body/jit(dynamic_update_index_in_dim)/dynamic_update_slice | solution.py:43
  68.9 2.7 %fusion.43 = (f32[128,512]{1,0:T(8,128)}, f32[5,128,512]{2,1,0:T(8,128)}) fusion(f32[6,128,512]{2,1,0:T(8,128)S(1)} %get-tuple-element.209, f32[6,128,512]{2,1,0:T(8,128)S(1)} %get-tuple-element.210, f32[6,128,512]{2,1,0:T(8,128)S(1)} %get-tuple-element.229, f32[6,128,512]{2,1,0:T(8,128)S(1)} %get-tuple-element.211, ...), kind=kLoop, calls=%fused_computation.10.clone.1 | loop fusion | flops 1572864 | bytes 8126464 | tf_op jit(solution)/shard_map/while/body/eval_jaxpr/reduce_sum | solution.py:36
  71.7 2.2 %bitcast_dynamic-update-slice_fusion.2 = (f32[12,128,512]{2,1,0:T(8,128)}, f32[128,512]{1,0:T(8,128)}, f32[1,128,512]{2,1,0:T(8,128)S(1)}) fusion(f32[12,128,512]{2,1,0:T(8,128)} %get-tuple-element.231, s32[]{:T(128)} %get-tuple-element.228, f32[6,128,512]{2,1,0:T(8,128)S(1)} %get-tuple-element.212, f32[1,128,512]{2,1,0:T(8,128)S(1)} %copy.39, ...), kind=kLoop, calls=%fused_computation.19.clone.1 | loop fusion | flops 786432 | bytes 2361857 | tf_op jit(solution)/shard_map/while/body/jit(dynamic_update_index_in_dim)/dynamic_update_slice | solution.py:43
  76.4 2.7 %fusion.43 = (f32[128,512]{1,0:T(8,128)}, f32[5,128,512]{2,1,0:T(8,128)}) fusion(f32[6,128,512]{2,1,0:T(8,128)S(1)} %get-tuple-element.209, f32[6,128,512]{2,1,0:T(8,128)S(1)} %get-tuple-element.210, f32[6,128,512]{2,1,0:T(8,128)S(1)} %get-tuple-element.229, f32[6,128,512]{2,1,0:T(8,128)S(1)} %get-tuple-element.211, ...), kind=kLoop, calls=%fused_computation.10.clone.1 | loop fusion | flops 1572864 | bytes 8126464 | tf_op jit(solution)/shard_map/while/body/eval_jaxpr/reduce_sum | solution.py:36
  79.1 2.2 %bitcast_dynamic-update-slice_fusion.2 = (f32[12,128,512]{2,1,0:T(8,128)}, f32[128,512]{1,0:T(8,128)}, f32[1,128,512]{2,1,0:T(8,128)S(1)}) fusion(f32[12,128,512]{2,1,0:T(8,128)} %get-tuple-element.231, s32[]{:T(128)} %get-tuple-element.228, f32[6,128,512]{2,1,0:T(8,128)S(1)} %get-tuple-element.212, f32[1,128,512]{2,1,0:T(8,128)S(1)} %copy.39, ...), kind=kLoop, calls=%fused_computation.19.clone.1 | loop fusion | flops 786432 | bytes 2361857 | tf_op jit(solution)/shard_map/while/body/jit(dynamic_update_index_in_dim)/dynamic_update_slice | solution.py:43
  83.9 2.7 %fusion.43 = (f32[128,512]{1,0:T(8,128)}, f32[5,128,512]{2,1,0:T(8,128)}) fusion(f32[6,128,512]{2,1,0:T(8,128)S(1)} %get-tuple-element.209, f32[6,128,512]{2,1,0:T(8,128)S(1)} %get-tuple-element.210, f32[6,128,512]{2,1,0:T(8,128)S(1)} %get-tuple-element.229, f32[6,128,512]{2,1,0:T(8,128)S(1)} %get-tuple-element.211, ...), kind=kLoop, calls=%fused_computation.10.clone.1 | loop fusion | flops 1572864 | bytes 8126464 | tf_op jit(solution)/shard_map/while/body/eval_jaxpr/reduce_sum | solution.py:36
  86.7 2.2 %bitcast_dynamic-update-slice_fusion.2 = (f32[12,128,512]{2,1,0:T(8,128)}, f32[128,512]{1,0:T(8,128)}, f32[1,128,512]{2,1,0:T(8,128)S(1)}) fusion(f32[12,128,512]{2,1,0:T(8,128)} %get-tuple-element.231, s32[]{:T(128)} %get-tuple-element.228, f32[6,128,512]{2,1,0:T(8,128)S(1)} %get-tuple-element.212, f32[1,128,512]{2,1,0:T(8,128)S(1)} %copy.39, ...), kind=kLoop, calls=%fused_computation.19.clone.1 | loop fusion | flops 786432 | bytes 2361857 | tf_op jit(solution)/shard_map/while/body/jit(dynamic_update_index_in_dim)/dynamic_update_slice | solution.py:43
  91.4 2.7 %fusion.43 = (f32[128,512]{1,0:T(8,128)}, f32[5,128,512]{2,1,0:T(8,128)}) fusion(f32[6,128,512]{2,1,0:T(8,128)S(1)} %get-tuple-element.209, f32[6,128,512]{2,1,0:T(8,128)S(1)} %get-tuple-element.210, f32[6,128,512]{2,1,0:T(8,128)S(1)} %get-tuple-element.229, f32[6,128,512]{2,1,0:T(8,128)S(1)} %get-tuple-element.211, ...), kind=kLoop, calls=%fused_computation.10.clone.1 | loop fusion | flops 1572864 | bytes 8126464 | tf_op jit(solution)/shard_map/while/body/eval_jaxpr/reduce_sum | solution.py:36
  94.1 2.2 %bitcast_dynamic-update-slice_fusion.2 = (f32[12,128,512]{2,1,0:T(8,128)}, f32[128,512]{1,0:T(8,128)}, f32[1,128,512]{2,1,0:T(8,128)S(1)}) fusion(f32[12,128,512]{2,1,0:T(8,128)} %get-tuple-element.231, s32[]{:T(128)} %get-tuple-element.228, f32[6,128,512]{2,1,0:T(8,128)S(1)} %get-tuple-element.212, f32[1,128,512]{2,1,0:T(8,128)S(1)} %copy.39, ...), kind=kLoop, calls=%fused_computation.19.clone.1 | loop fusion | flops 786432 | bytes 2361857 | tf_op jit(solution)/shard_map/while/body/jit(dynamic_update_index_in_dim)/dynamic_update_slice | solution.py:43
  98.9 2.7 %fusion.43 = (f32[128,512]{1,0:T(8,128)}, f32[5,128,512]{2,1,0:T(8,128)}) fusion(f32[6,128,512]{2,1,0:T(8,128)S(1)} %get-tuple-element.209, f32[6,128,512]{2,1,0:T(8,128)S(1)} %get-tuple-element.210, f32[6,128,512]{2,1,0:T(8,128)S(1)} %get-tuple-element.229, f32[6,128,512]{2,1,0:T(8,128)S(1)} %get-tuple-element.211, ...), kind=kLoop, calls=%fused_computation.10.clone.1 | loop fusion | flops 1572864 | bytes 8126464 | tf_op jit(solution)/shard_map/while/body/eval_jaxpr/reduce_sum | solution.py:36
  101.6 2.3 %bitcast_dynamic-update-slice_fusion.2 = (f32[12,128,512]{2,1,0:T(8,128)}, f32[128,512]{1,0:T(8,128)}, f32[1,128,512]{2,1,0:T(8,128)S(1)}) fusion(f32[12,128,512]{2,1,0:T(8,128)} %get-tuple-element.231, s32[]{:T(128)} %get-tuple-element.228, f32[6,128,512]{2,1,0:T(8,128)S(1)} %get-tuple-element.212, f32[1,128,512]{2,1,0:T(8,128)S(1)} %copy.39, ...), kind=kLoop, calls=%fused_computation.19.clone.1 | loop fusion | flops 786432 | bytes 2361857 | tf_op jit(solution)/shard_map/while/body/jit(dynamic_update_index_in_dim)/dynamic_update_slice | solution.py:43
  106.4 2.7 %fusion.43 = (f32[128,512]{1,0:T(8,128)}, f32[5,128,512]{2,1,0:T(8,128)}) fusion(f32[6,128,512]{2,1,0:T(8,128)S(1)} %get-tuple-element.209, f32[6,128,512]{2,1,0:T(8,128)S(1)} %get-tuple-element.210, f32[6,128,512]{2,1,0:T(8,128)S(1)} %get-tuple-element.229, f32[6,128,512]{2,1,0:T(8,128)S(1)} %get-tuple-element.211, ...), kind=kLoop, calls=%fused_computation.10.clone.1 | loop fusion | flops 1572864 | bytes 8126464 | tf_op jit(solution)/shard_map/while/body/eval_jaxpr/reduce_sum | solution.py:36
  109.2 2.2 %bitcast_dynamic-update-slice_fusion.2 = (f32[12,128,512]{2,1,0:T(8,128)}, f32[128,512]{1,0:T(8,128)}, f32[1,128,512]{2,1,0:T(8,128)S(1)}) fusion(f32[12,128,512]{2,1,0:T(8,128)} %get-tuple-element.231, s32[]{:T(128)} %get-tuple-element.228, f32[6,128,512]{2,1,0:T(8,128)S(1)} %get-tuple-element.212, f32[1,128,512]{2,1,0:T(8,128)S(1)} %copy.39, ...), kind=kLoop, calls=%fused_computation.19.clone.1 | loop fusion | flops 786432 | bytes 2361857 | tf_op jit(solution)/shard_map/while/body/jit(dynamic_update_index_in_dim)/dynamic_update_slice | solution.py:43
  113.9 2.7 %fusion.43 = (f32[128,512]{1,0:T(8,128)}, f32[5,128,512]{2,1,0:T(8,128)}) fusion(f32[6,128,512]{2,1,0:T(8,128)S(1)} %get-tuple-element.209, f32[6,128,512]{2,1,0:T(8,128)S(1)} %get-tuple-element.210, f32[6,128,512]{2,1,0:T(8,128)S(1)} %get-tuple-element.229, f32[6,128,512]{2,1,0:T(8,128)S(1)} %get-tuple-element.211, ...), kind=kLoop, calls=%fused_computation.10.clone.1 | loop fusion | flops 1572864 | bytes 8126464 | tf_op jit(solution)/shard_map/while/body/eval_jaxpr/reduce_sum | solution.py:36
  116.7 2.2 %bitcast_dynamic-update-slice_fusion.2 = (f32[12,128,512]{2,1,0:T(8,128)}, f32[128,512]{1,0:T(8,128)}, f32[1,128,512]{2,1,0:T(8,128)S(1)}) fusion(f32[12,128,512]{2,1,0:T(8,128)} %get-tuple-element.231, s32[]{:T(128)} %get-tuple-element.228, f32[6,128,512]{2,1,0:T(8,128)S(1)} %get-tuple-element.212, f32[1,128,512]{2,1,0:T(8,128)S(1)} %copy.39, ...), kind=kLoop, calls=%fused_computation.19.clone.1 | loop fusion | flops 786432 | bytes 2361857 | tf_op jit(solution)/shard_map/while/body/jit(dynamic_update_index_in_dim)/dynamic_update_slice | solution.py:43
  121.4 2.7 %fusion.43 = (f32[128,512]{1,0:T(8,128)}, f32[5,128,512]{2,1,0:T(8,128)}) fusion(f32[6,128,512]{2,1,0:T(8,128)S(1)} %get-tuple-element.209, f32[6,128,512]{2,1,0:T(8,128)S(1)} %get-tuple-element.210, f32[6,128,512]{2,1,0:T(8,128)S(1)} %get-tuple-element.229, f32[6,128,512]{2,1,0:T(8,128)S(1)} %get-tuple-element.211, ...), kind=kLoop, calls=%fused_computation.10.clone.1 | loop fusion | flops 1572864 | bytes 8126464 | tf_op jit(solution)/shard_map/while/body/eval_jaxpr/reduce_sum | solution.py:36
  124.2 2.2 %bitcast_dynamic-update-slice_fusion.2 = (f32[12,128,512]{2,1,0:T(8,128)}, f32[128,512]{1,0:T(8,128)}, f32[1,128,512]{2,1,0:T(8,128)S(1)}) fusion(f32[12,128,512]{2,1,0:T(8,128)} %get-tuple-element.231, s32[]{:T(128)} %get-tuple-element.228, f32[6,128,512]{2,1,0:T(8,128)S(1)} %get-tuple-element.212, f32[1,128,512]{2,1,0:T(8,128)S(1)} %copy.39, ...), kind=kLoop, calls=%fused_computation.19.clone.1 | loop fusion | flops 786432 | bytes 2361857 | tf_op jit(solution)/shard_map/while/body/jit(dynamic_update_index_in_dim)/dynamic_update_slice | solution.py:43
  128.9 2.7 %fusion.43 = (f32[128,512]{1,0:T(8,128)}, f32[5,128,512]{2,1,0:T(8,128)}) fusion(f32[6,128,512]{2,1,0:T(8,128)S(1)} %get-tuple-element.209, f32[6,128,512]{2,1,0:T(8,128)S(1)} %get-tuple-element.210, f32[6,128,512]{2,1,0:T(8,128)S(1)} %get-tuple-element.229, f32[6,128,512]{2,1,0:T(8,128)S(1)} %get-tuple-element.211, ...), kind=kLoop, calls=%fused_computation.10.clone.1 | loop fusion | flops 1572864 | bytes 8126464 | tf_op jit(solution)/shard_map/while/body/eval_jaxpr/reduce_sum | solution.py:36
  131.6 2.2 %bitcast_dynamic-update-slice_fusion.2 = (f32[12,128,512]{2,1,0:T(8,128)}, f32[128,512]{1,0:T(8,128)}, f32[1,128,512]{2,1,0:T(8,128)S(1)}) fusion(f32[12,128,512]{2,1,0:T(8,128)} %get-tuple-element.231, s32[]{:T(128)} %get-tuple-element.228, f32[6,128,512]{2,1,0:T(8,128)S(1)} %get-tuple-element.212, f32[1,128,512]{2,1,0:T(8,128)S(1)} %copy.39, ...), kind=kLoop, calls=%fused_computation.19.clone.1 | loop fusion | flops 786432 | bytes 2361857 | tf_op jit(solution)/shard_map/while/body/jit(dynamic_update_index_in_dim)/dynamic_update_slice | solution.py:43
  137.0 3.4 %all-to-all-start.1 = ((f32[8,8,384]{2,1,0:T(8,128)}), f32[8,8,384]{2,1,0:T(8,128)S(1)}, u32[]{:S(2)}, u32[]{:S(2)}) async-start(f32[8,8,384]{2,1,0:T(8,128)} %bitcast.5), calls=%async_computation.1 | async-start | bytes 196608 | tf_op jit(solution)/shard_map/all_to_all | solution.py:118
  140.6 4.9 %all-to-all-done.1 = f32[8,8,384]{2,1,0:T(8,128)S(1)} async-done(((f32[8,8,384]{2,1,0:T(8,128)}), f32[8,8,384]{2,1,0:T(8,128)S(1)}, u32[]{:S(2)}, u32[]{:S(2)}) %all-to-all-start.1) | async-done | bytes 98336 | tf_op jit(solution)/shard_map/all_to_all | solution.py:118
  146.8 18.7 %psum.7 = f32[6,3,64]{2,0,1:T(8,128)S(1)} all-reduce(f32[6,3,64]{2,0,1:T(8,128)S(1)} %bitcast.74), channel_id=1, replica_groups=mesh['loan'=8,'path'=4] {'path'}, use_global_device_ids=true, to_apply=%region_7.8 | all-reduce | flops 1152 | bytes 9216 | tf_op jit(solution)/shard_map/psum | solution.py:139
  (184 shorter events, 51.6 us)
Async XLA Ops:
  7.2 14.3 %copy-start.9 = (s32[2,32]{1,0:T(2,128)S(1)}, s32[2,32]{1,0:T(2,128)}, u32[]{:S(2)}) copy-start(s32[2,32]{1,0:T(2,128)} %param.14) | copy-start | bytes 772
  7.2 14.3 %copy-start.5 = (s32[64,6]{0,1:T(8,128)S(1)}, s32[64,6]{0,1:T(8,128)}, u32[]{:S(2)}) copy-start(s32[64,6]{0,1:T(8,128)} %param.23) | copy-start | bytes 4612
  7.2 14.4 %copy-start.7 = (s32[512]{0:T(512)S(1)}, s32[512]{0:T(512)}, u32[]{:S(2)}) copy-start(s32[512]{0:T(512)} %param.15) | copy-start | bytes 6148
  7.2 14.6 %copy-start.6 = (s32[512]{0:T(512)S(1)}, s32[512]{0:T(512)}, u32[]{:S(2)}) copy-start(s32[512]{0:T(512)} %param.18) | copy-start | bytes 6148
  7.2 14.6 %copy-start.8 = (f32[512]{0:T(512)S(1)}, f32[512]{0:T(512)}, u32[]{:S(2)}) copy-start(f32[512]{0:T(512)} %param.20) | copy-start | bytes 6148
  7.2 31.6 %all-gather.2.cloned.1.call-start = ((), (), s32[]{:S(2)}) async-start(), calls=%async_computation.3 | async-start | bytes 1916928 | tf_op jit(solution)/shard_map/all_gather | solution.py:73
  13.2 9.8 %all-to-all-start = ((f32[8,8,1]{1,2,0:T(1,128)}), f32[8,8,1]{1,2,0:T(1,128)S(1)}, u32[]{:S(2)}, u32[]{:S(2)}) async-start(f32[8,8,1]{1,2,0:T(1,128)} %bitcast), calls=%async_computation | async-start | bytes 8192 | tf_op jit(solution)/shard_map/all_to_all | solution.py:120
  23.0 7.9 %all-to-all-start.2 = ((f32[8,8,1]{1,2,0:T(1,128)}), f32[8,8,1]{1,2,0:T(1,128)S(1)}, u32[]{:S(2)}, u32[]{:S(2)}) async-start(f32[8,8,1]{1,2,0:T(1,128)} %bitcast.10), calls=%async_computation.2 | async-start | bytes 8192 | tf_op jit(solution)/shard_map/all_to_all | solution.py:119
  46.4 2.8 %copy-start = (f32[6,128,512]{2,1,0:T(8,128)}, f32[6,128,512]{2,1,0:T(8,128)S(1)}, u32[]{:S(2)}) copy-start(f32[6,128,512]{2,1,0:T(8,128)S(1)} %get-tuple-element.211) | copy-start | bytes 4718596 | tf_op jit(solution)/shard_map/while
  53.9 2.8 %copy-start = (f32[6,128,512]{2,1,0:T(8,128)}, f32[6,128,512]{2,1,0:T(8,128)S(1)}, u32[]{:S(2)}) copy-start(f32[6,128,512]{2,1,0:T(8,128)S(1)} %get-tuple-element.211) | copy-start | bytes 4718596 | tf_op jit(solution)/shard_map/while
  56.6 2.2 %copy-start.1 = (f32[5,128,512]{2,1,0:T(8,128)S(1)}, f32[5,128,512]{2,1,0:T(8,128)}, u32[]{:S(2)}) copy-start(f32[5,128,512]{2,1,0:T(8,128)} %get-tuple-element.213) | copy-start | bytes 3932164 | tf_op jit(solution)/shard_map/while
  61.4 2.8 %copy-start = (f32[6,128,512]{2,1,0:T(8,128)}, f32[6,128,512]{2,1,0:T(8,128)S(1)}, u32[]{:S(2)}) copy-start(f32[6,128,512]{2,1,0:T(8,128)S(1)} %get-tuple-element.211) | copy-start | bytes 4718596 | tf_op jit(solution)/shard_map/while
  64.1 2.2 %copy-start.1 = (f32[5,128,512]{2,1,0:T(8,128)S(1)}, f32[5,128,512]{2,1,0:T(8,128)}, u32[]{:S(2)}) copy-start(f32[5,128,512]{2,1,0:T(8,128)} %get-tuple-element.213) | copy-start | bytes 3932164 | tf_op jit(solution)/shard_map/while
  68.9 2.8 %copy-start = (f32[6,128,512]{2,1,0:T(8,128)}, f32[6,128,512]{2,1,0:T(8,128)S(1)}, u32[]{:S(2)}) copy-start(f32[6,128,512]{2,1,0:T(8,128)S(1)} %get-tuple-element.211) | copy-start | bytes 4718596 | tf_op jit(solution)/shard_map/while
  71.7 2.2 %copy-start.1 = (f32[5,128,512]{2,1,0:T(8,128)S(1)}, f32[5,128,512]{2,1,0:T(8,128)}, u32[]{:S(2)}) copy-start(f32[5,128,512]{2,1,0:T(8,128)} %get-tuple-element.213) | copy-start | bytes 3932164 | tf_op jit(solution)/shard_map/while
  76.4 2.8 %copy-start = (f32[6,128,512]{2,1,0:T(8,128)}, f32[6,128,512]{2,1,0:T(8,128)S(1)}, u32[]{:S(2)}) copy-start(f32[6,128,512]{2,1,0:T(8,128)S(1)} %get-tuple-element.211) | copy-start | bytes 4718596 | tf_op jit(solution)/shard_map/while
  79.1 2.2 %copy-start.1 = (f32[5,128,512]{2,1,0:T(8,128)S(1)}, f32[5,128,512]{2,1,0:T(8,128)}, u32[]{:S(2)}) copy-start(f32[5,128,512]{2,1,0:T(8,128)} %get-tuple-element.213) | copy-start | bytes 3932164 | tf_op jit(solution)/shard_map/while
  83.9 2.8 %copy-start = (f32[6,128,512]{2,1,0:T(8,128)}, f32[6,128,512]{2,1,0:T(8,128)S(1)}, u32[]{:S(2)}) copy-start(f32[6,128,512]{2,1,0:T(8,128)S(1)} %get-tuple-element.211) | copy-start | bytes 4718596 | tf_op jit(solution)/shard_map/while
  86.7 2.2 %copy-start.1 = (f32[5,128,512]{2,1,0:T(8,128)S(1)}, f32[5,128,512]{2,1,0:T(8,128)}, u32[]{:S(2)}) copy-start(f32[5,128,512]{2,1,0:T(8,128)} %get-tuple-element.213) | copy-start | bytes 3932164 | tf_op jit(solution)/shard_map/while
  91.4 2.8 %copy-start = (f32[6,128,512]{2,1,0:T(8,128)}, f32[6,128,512]{2,1,0:T(8,128)S(1)}, u32[]{:S(2)}) copy-start(f32[6,128,512]{2,1,0:T(8,128)S(1)} %get-tuple-element.211) | copy-start | bytes 4718596 | tf_op jit(solution)/shard_map/while
  94.1 2.2 %copy-start.1 = (f32[5,128,512]{2,1,0:T(8,128)S(1)}, f32[5,128,512]{2,1,0:T(8,128)}, u32[]{:S(2)}) copy-start(f32[5,128,512]{2,1,0:T(8,128)} %get-tuple-element.213) | copy-start | bytes 3932164 | tf_op jit(solution)/shard_map/while
  98.9 2.8 %copy-start = (f32[6,128,512]{2,1,0:T(8,128)}, f32[6,128,512]{2,1,0:T(8,128)S(1)}, u32[]{:S(2)}) copy-start(f32[6,128,512]{2,1,0:T(8,128)S(1)} %get-tuple-element.211) | copy-start | bytes 4718596 | tf_op jit(solution)/shard_map/while
  101.6 2.3 %copy-start.1 = (f32[5,128,512]{2,1,0:T(8,128)S(1)}, f32[5,128,512]{2,1,0:T(8,128)}, u32[]{:S(2)}) copy-start(f32[5,128,512]{2,1,0:T(8,128)} %get-tuple-element.213) | copy-start | bytes 3932164 | tf_op jit(solution)/shard_map/while
  106.4 2.8 %copy-start = (f32[6,128,512]{2,1,0:T(8,128)}, f32[6,128,512]{2,1,0:T(8,128)S(1)}, u32[]{:S(2)}) copy-start(f32[6,128,512]{2,1,0:T(8,128)S(1)} %get-tuple-element.211) | copy-start | bytes 4718596 | tf_op jit(solution)/shard_map/while
  109.2 2.2 %copy-start.1 = (f32[5,128,512]{2,1,0:T(8,128)S(1)}, f32[5,128,512]{2,1,0:T(8,128)}, u32[]{:S(2)}) copy-start(f32[5,128,512]{2,1,0:T(8,128)} %get-tuple-element.213) | copy-start | bytes 3932164 | tf_op jit(solution)/shard_map/while
  113.9 2.8 %copy-start = (f32[6,128,512]{2,1,0:T(8,128)}, f32[6,128,512]{2,1,0:T(8,128)S(1)}, u32[]{:S(2)}) copy-start(f32[6,128,512]{2,1,0:T(8,128)S(1)} %get-tuple-element.211) | copy-start | bytes 4718596 | tf_op jit(solution)/shard_map/while
  116.7 2.2 %copy-start.1 = (f32[5,128,512]{2,1,0:T(8,128)S(1)}, f32[5,128,512]{2,1,0:T(8,128)}, u32[]{:S(2)}) copy-start(f32[5,128,512]{2,1,0:T(8,128)} %get-tuple-element.213) | copy-start | bytes 3932164 | tf_op jit(solution)/shard_map/while
  121.4 2.8 %copy-start = (f32[6,128,512]{2,1,0:T(8,128)}, f32[6,128,512]{2,1,0:T(8,128)S(1)}, u32[]{:S(2)}) copy-start(f32[6,128,512]{2,1,0:T(8,128)S(1)} %get-tuple-element.211) | copy-start | bytes 4718596 | tf_op jit(solution)/shard_map/while
  124.2 2.2 %copy-start.1 = (f32[5,128,512]{2,1,0:T(8,128)S(1)}, f32[5,128,512]{2,1,0:T(8,128)}, u32[]{:S(2)}) copy-start(f32[5,128,512]{2,1,0:T(8,128)} %get-tuple-element.213) | copy-start | bytes 3932164 | tf_op jit(solution)/shard_map/while
  128.9 2.8 %copy-start = (f32[6,128,512]{2,1,0:T(8,128)}, f32[6,128,512]{2,1,0:T(8,128)S(1)}, u32[]{:S(2)}) copy-start(f32[6,128,512]{2,1,0:T(8,128)S(1)} %get-tuple-element.211) | copy-start | bytes 4718596 | tf_op jit(solution)/shard_map/while
  131.6 2.2 %copy-start.1 = (f32[5,128,512]{2,1,0:T(8,128)S(1)}, f32[5,128,512]{2,1,0:T(8,128)}, u32[]{:S(2)}) copy-start(f32[5,128,512]{2,1,0:T(8,128)} %get-tuple-element.213) | copy-start | bytes 3932164 | tf_op jit(solution)/shard_map/while
  137.0 8.5 %all-to-all-start.1 = ((f32[8,8,384]{2,1,0:T(8,128)}), f32[8,8,384]{2,1,0:T(8,128)S(1)}, u32[]{:S(2)}, u32[]{:S(2)}) async-start(f32[8,8,384]{2,1,0:T(8,128)} %bitcast.5), calls=%async_computation.1 | async-start | bytes 196608 | tf_op jit(solution)/shard_map/all_to_all | solution.py:118
  (4 other events, 4.2 us)
Sparse Core Ops, SparseCore 0:
  9.9 28.8 all-gather.1
where the time goes:
time: 174 us; the launch traced here: 173 us
  other arithmetic  81.9 us (47%)
  local copies, waits for them, and re-layouts  24 us (14%)
  blocking collectives  18.7 us (11%)
  waiting for transfers between devices  17.3 us (10%)
  between operations  14.2 us (8%)
  starting transfers between devices  11.9 us (7%)
  matrix products  4.24 us (2%)
    reduce_sum x12, other arithmetic, month_step(): first_state = state[0] * stay_rate[0] + jnp.sum(backward[1:], axis=0)  32.9 us
    dynamic_update_slice x12, other arithmetic, roll_months(): state_pair, history = lax.scan(month_step, (start_state, loss_start), level)  26.6 us
    psum x1, blocking collectives, shards(): expected_loss = lax.psum(partial_value, 'path') / path_count  18.7 us
    sub x12, other arithmetic, month_step(): stay_rate = (1.0 - roll_rate) * (1.0 - cure_rate)  14.8 us
    dynamic_slice x24, local copies, waits for them, and re-layouts, roll_months(): state_pair, history = lax.scan(month_step, (start_state, loss_start), level)  13.2 us
    all_gather x1, waiting for transfers between devices, shards(): shard = lax.all_gather(price_moves, 'loan', axis=1, tiled=True)  6.63 us
    all_to_all x1, starting transfers between devices, shards(): lax.all_to_all(outgoing[2], 'loan', split_axis=0, concat_axis=0, tiled=True)  5.2 us
    all_to_all x1, waiting for transfers between devices, shards(): lax.all_to_all(outgoing[0], 'loan', split_axis=0, concat_axis=0, tiled=True)  4.94 us
  transfers between devices with their start and end apart: 4, of which 4 were waited for; matrix products, arithmetic and copies ran while one was open for 5% of the time, Pallas kernels for 0%

commit v1 on v0

--- a/solution.py
+++ b/solution.py
@@ -5,6 +5,11 @@
 
 BLOCK = 256
 stress_scale = 0.3
+
+
+def gather_and_add(x, axis):
+    parts = lax.all_gather(x, axis)
+    return jnp.sum(parts, axis=0)
 
 
 def roll_months(
@@ -136,7 +141,7 @@
     height = (detach - attach).T[:, :, None, None]
     shares = jnp.clip((ratio[None] - lower) / height, 0.0, 1.0)
     partial_value = jnp.sum(shares, axis=3).transpose(0, 2, 1)
-    expected_loss = lax.psum(partial_value, "path") / path_count
+    expected_loss = gather_and_add(partial_value, "path") / path_count
     return (expected_loss, shares[:, :, -1, :])
 
 

time: 174 us -> 169 us (0.971)
  blocking collectives: 18.7 us -> 13.2 us
    psum x1 -> x0, blocking collectives: 18.7 us -> none  [shards(): expected_loss = lax.psum(partial_value, 'path') / path_count]
    all_gather x0 -> x1, blocking collectives: none -> 13.2 us  [gather_and_add(): parts = lax.all_gather(x, axis)]
where the time goes in v1:
time: 169 us; the launch traced here: 167 us
  other arithmetic  82.5 us (49%)
  local copies, waits for them, and re-layouts  23.4 us (14%)
  waiting for transfers between devices  17.3 us (10%)
  between operations  14.2 us (8%)
  blocking collectives  13.2 us (8%)
  starting transfers between devices  11.9 us (7%)
  matrix products  4.24 us (3%)
    reduce_sum x12, other arithmetic, month_step(): first_state = state[0] * stay_rate[0] + jnp.sum(backward[1:], axis=0)  32.9 us
    dynamic_update_slice x12, other arithmetic, roll_months(): state_pair, history = lax.scan(month_step, (start_state, loss_start), level)  26.6 us
    sub x12, other arithmetic, month_step(): stay_rate = (1.0 - roll_rate) * (1.0 - cure_rate)  14.8 us
    dynamic_slice x24, local copies, waits for them, and re-layouts, roll_months(): state_pair, history = lax.scan(month_step, (start_state, loss_start), level)  13.2 us
    all_gather x1, blocking collectives, gather_and_add(): parts = lax.all_gather(x, axis)  13.2 us
    all_gather x1, waiting for transfers between devices, shards(): shard = lax.all_gather(price_moves, 'loan', axis=1, tiled=True)  6.63 us
    all_to_all x1, starting transfers between devices, shards(): lax.all_to_all(outgoing[2], 'loan', split_axis=0, concat_axis=0, tiled=True)  5.2 us
    all_to_all x1, waiting for transfers between devices, shards(): lax.all_to_all(outgoing[0], 'loan', split_axis=0, concat_axis=0, tiled=True)  4.94 us
  transfers between devices with their start and end apart: 4, of which 4 were waited for; matrix products, arithmetic and copies ran while one was open for 5% of the time, Pallas kernels for 0%

profile of v1, /device:TPU:0, one launch (start us, length us, event | category | flops | bytes accessed | tf_op | source)
XLA Modules:
  0.0 167.5 jit_solution(10723421372465359828)
XLA Ops:
  13.2 5.2 %all-to-all-start = ((f32[8,8,1]{1,2,0:T(1,128)}), f32[8,8,1]{1,2,0:T(1,128)S(1)}, u32[]{:S(2)}, u32[]{:S(2)}) async-start(f32[8,8,1]{1,2,0:T(1,128)} %bitcast), calls=%async_computation | async-start | bytes 8192 | tf_op jit(solution)/shard_map/all_to_all | solution.py:125
  23.0 3.3 %all-to-all-start.2 = ((f32[8,8,1]{1,2,0:T(1,128)}), f32[8,8,1]{1,2,0:T(1,128)S(1)}, u32[]{:S(2)}, u32[]{:S(2)}) async-start(f32[8,8,1]{1,2,0:T(1,128)} %bitcast.10), calls=%async_computation.2 | async-start | bytes 8192 | tf_op jit(solution)/shard_map/all_to_all | solution.py:124
  26.5 4.4 %all-to-all-done.2 = f32[8,8,1]{1,2,0:T(1,128)S(1)} async-done(((f32[8,8,1]{1,2,0:T(1,128)}), f32[8,8,1]{1,2,0:T(1,128)S(1)}, u32[]{:S(2)}, u32[]{:S(2)}) %all-to-all-start.2) | async-done | bytes 288 | tf_op jit(solution)/shard_map/all_to_all | solution.py:124
  32.2 6.6 %all-gather.3.cloned.1.call-done = bf16[12,416,128]{2,0,1:T(8,128)(2,1)} async-done(((bf16[12,52,128]{2,0,1:T(8,128)(2,1)}), bf16[12,416,128]{2,0,1:T(8,128)(2,1)}) %all-gather.3.cloned.1.call-update) | async-done | bytes 1277968 | tf_op jit(solution)/shard_map/all_gather | solution.py:78
  38.8 2.5 %fusion.9 = f32[512,12,128]{2,0,1:T(8,128)S(1)} fusion(bf16[12,416,128]{2,0,1:T(8,128)(2,1)} %all-gather.3.cloned.1.call-done, s32[512]{0:T(512)S(1)} %select_reduce_fusion), kind=kOutput, calls=%fused_computation.28 | convolution fusion | flops 654524416 | bytes 4425728 | tf_op jit(solution)/shard_map/mrp,rl->mpl/dot_general | solution.py:82
  44.1 89.9 %while.15 = (s32[]{:T(128)}, f32[6,128,512]{2,1,0:T(8,128)S(1)}, f32[128,512]{1,0:T(8,128)}, f32[12,128,512]{2,1,0:T(8,128)}, f32[2,6]{1,0:T(2,128)S(1)}, /*inde...) while((s32[]{:T(128)}, f32[6,128,512]{2,1,0:T(8,128)S(1)}, ...), condition=%wide.region_5.6_spmd.clone, body=%wide.region_3.5_spmd.clone.sunk | while | flops 8257539 | bytes 34343880 | solution.py:48
  46.4 2.7 %fusion.43 = (f32[128,512]{1,0:T(8,128)}, f32[5,128,512]{2,1,0:T(8,128)}) fusion(f32[6,128,512]{2,1,0:T(8,128)S(1)} %get-tuple-element.205, f32[6,128,512]{2,1,0:T(8,128)S(1)} %get-tuple-element.206, f32[6,128,512]{2,1,0:T(8,128)S(1)} %get-tuple-element.225, f32[6,128,512]{2,1,0:T(8,128)S(1)} %get-tuple-element.207, ...), kind=kLoop, calls=%fused_computation.10.clone.1 | loop fusion | flops 1572864 | bytes 8126464 | tf_op jit(solution)/shard_map/while/body/eval_jaxpr/reduce_sum | solution.py:41
  53.9 2.7 %fusion.43 = (f32[128,512]{1,0:T(8,128)}, f32[5,128,512]{2,1,0:T(8,128)}) fusion(f32[6,128,512]{2,1,0:T(8,128)S(1)} %get-tuple-element.205, f32[6,128,512]{2,1,0:T(8,128)S(1)} %get-tuple-element.206, f32[6,128,512]{2,1,0:T(8,128)S(1)} %get-tuple-element.225, f32[6,128,512]{2,1,0:T(8,128)S(1)} %get-tuple-element.207, ...), kind=kLoop, calls=%fused_computation.10.clone.1 | loop fusion | flops 1572864 | bytes 8126464 | tf_op jit(solution)/shard_map/while/body/eval_jaxpr/reduce_sum | solution.py:41
  56.6 2.2 %bitcast_dynamic-update-slice_fusion.2 = (f32[12,128,512]{2,1,0:T(8,128)}, f32[128,512]{1,0:T(8,128)}, f32[1,128,512]{2,1,0:T(8,128)S(1)}) fusion(f32[12,128,512]{2,1,0:T(8,128)} %get-tuple-element.227, s32[]{:T(128)} %get-tuple-element.224, f32[6,128,512]{2,1,0:T(8,128)S(1)} %get-tuple-element.208, f32[1,128,512]{2,1,0:T(8,128)S(1)} %copy.39, ...), kind=kLoop, calls=%fused_computation.19.clone.1 | loop fusion | flops 786432 | bytes 2361857 | tf_op jit(solution)/shard_map/while/body/jit(dynamic_update_index_in_dim)/dynamic_update_slice | solution.py:48
  61.4 2.7 %fusion.43 = (f32[128,512]{1,0:T(8,128)}, f32[5,128,512]{2,1,0:T(8,128)}) fusion(f32[6,128,512]{2,1,0:T(8,128)S(1)} %get-tuple-element.205, f32[6,128,512]{2,1,0:T(8,128)S(1)} %get-tuple-element.206, f32[6,128,512]{2,1,0:T(8,128)S(1)} %get-tuple-element.225, f32[6,128,512]{2,1,0:T(8,128)S(1)} %get-tuple-element.207, ...), kind=kLoop, calls=%fused_computation.10.clone.1 | loop fusion | flops 1572864 | bytes 8126464 | tf_op jit(solution)/shard_map/while/body/eval_jaxpr/reduce_sum | solution.py:41
  64.1 2.2 %bitcast_dynamic-update-slice_fusion.2 = (f32[12,128,512]{2,1,0:T(8,128)}, f32[128,512]{1,0:T(8,128)}, f32[1,128,512]{2,1,0:T(8,128)S(1)}) fusion(f32[12,128,512]{2,1,0:T(8,128)} %get-tuple-element.227, s32[]{:T(128)} %get-tuple-element.224, f32[6,128,512]{2,1,0:T(8,128)S(1)} %get-tuple-element.208, f32[1,128,512]{2,1,0:T(8,128)S(1)} %copy.39, ...), kind=kLoop, calls=%fused_computation.19.clone.1 | loop fusion | flops 786432 | bytes 2361857 | tf_op jit(solution)/shard_map/while/body/jit(dynamic_update_index_in_dim)/dynamic_update_slice | solution.py:48
  68.9 2.7 %fusion.43 = (f32[128,512]{1,0:T(8,128)}, f32[5,128,512]{2,1,0:T(8,128)}) fusion(f32[6,128,512]{2,1,0:T(8,128)S(1)} %get-tuple-element.205, f32[6,128,512]{2,1,0:T(8,128)S(1)} %get-tuple-element.206, f32[6,128,512]{2,1,0:T(8,128)S(1)} %get-tuple-element.225, f32[6,128,512]{2,1,0:T(8,128)S(1)} %get-tuple-element.207, ...), kind=kLoop, calls=%fused_computation.10.clone.1 | loop fusion | flops 1572864 | bytes 8126464 | tf_op jit(solution)/shard_map/while/body/eval_jaxpr/reduce_sum | solution.py:41
  71.7 2.2 %bitcast_dynamic-update-slice_fusion.2 = (f32[12,128,512]{2,1,0:T(8,128)}, f32[128,512]{1,0:T(8,128)}, f32[1,128,512]{2,1,0:T(8,128)S(1)}) fusion(f32[12,128,512]{2,1,0:T(8,128)} %get-tuple-element.227, s32[]{:T(128)} %get-tuple-element.224, f32[6,128,512]{2,1,0:T(8,128)S(1)} %get-tuple-element.208, f32[1,128,512]{2,1,0:T(8,128)S(1)} %copy.39, ...), kind=kLoop, calls=%fused_computation.19.clone.1 | loop fusion | flops 786432 | bytes 2361857 | tf_op jit(solution)/shard_map/while/body/jit(dynamic_update_index_in_dim)/dynamic_update_slice | solution.py:48
  76.4 2.7 %fusion.43 = (f32[128,512]{1,0:T(8,128)}, f32[5,128,512]{2,1,0:T(8,128)}) fusion(f32[6,128,512]{2,1,0:T(8,128)S(1)} %get-tuple-element.205, f32[6,128,512]{2,1,0:T(8,128)S(1)} %get-tuple-element.206, f32[6,128,512]{2,1,0:T(8,128)S(1)} %get-tuple-element.225, f32[6,128,512]{2,1,0:T(8,128)S(1)} %get-tuple-element.207, ...), kind=kLoop, calls=%fused_computation.10.clone.1 | loop fusion | flops 1572864 | bytes 8126464 | tf_op jit(solution)/shard_map/while/body/eval_jaxpr/reduce_sum | solution.py:41
  79.1 2.2 %bitcast_dynamic-update-slice_fusion.2 = (f32[12,128,512]{2,1,0:T(8,128)}, f32[128,512]{1,0:T(8,128)}, f32[1,128,512]{2,1,0:T(8,128)S(1)}) fusion(f32[12,128,512]{2,1,0:T(8,128)} %get-tuple-element.227, s32[]{:T(128)} %get-tuple-element.224, f32[6,128,512]{2,1,0:T(8,128)S(1)} %get-tuple-element.208, f32[1,128,512]{2,1,0:T(8,128)S(1)} %copy.39, ...), kind=kLoop, calls=%fused_computation.19.clone.1 | loop fusion | flops 786432 | bytes 2361857 | tf_op jit(solution)/shard_map/while/body/jit(dynamic_update_index_in_dim)/dynamic_update_slice | solution.py:48
  83.9 2.7 %fusion.43 = (f32[128,512]{1,0:T(8,128)}, f32[5,128,512]{2,1,0:T(8,128)}) fusion(f32[6,128,512]{2,1,0:T(8,128)S(1)} %get-tuple-element.205, f32[6,128,512]{2,1,0:T(8,128)S(1)} %get-tuple-element.206, f32[6,128,512]{2,1,0:T(8,128)S(1)} %get-tuple-element.225, f32[6,128,512]{2,1,0:T(8,128)S(1)} %get-tuple-element.207, ...), kind=kLoop, calls=%fused_computation.10.clone.1 | loop fusion | flops 1572864 | bytes 8126464 | tf_op jit(solution)/shard_map/while/body/eval_jaxpr/reduce_sum | solution.py:41
  86.7 2.2 %bitcast_dynamic-update-slice_fusion.2 = (f32[12,128,512]{2,1,0:T(8,128)}, f32[128,512]{1,0:T(8,128)}, f32[1,128,512]{2,1,0:T(8,128)S(1)}) fusion(f32[12,128,512]{2,1,0:T(8,128)} %get-tuple-element.227, s32[]{:T(128)} %get-tuple-element.224, f32[6,128,512]{2,1,0:T(8,128)S(1)} %get-tuple-element.208, f32[1,128,512]{2,1,0:T(8,128)S(1)} %copy.39, ...), kind=kLoop, calls=%fused_computation.19.clone.1 | loop fusion | flops 786432 | bytes 2361857 | tf_op jit(solution)/shard_map/while/body/jit(dynamic_update_index_in_dim)/dynamic_update_slice | solution.py:48
  91.4 2.7 %fusion.43 = (f32[128,512]{1,0:T(8,128)}, f32[5,128,512]{2,1,0:T(8,128)}) fusion(f32[6,128,512]{2,1,0:T(8,128)S(1)} %get-tuple-element.205, f32[6,128,512]{2,1,0:T(8,128)S(1)} %get-tuple-element.206, f32[6,128,512]{2,1,0:T(8,128)S(1)} %get-tuple-element.225, f32[6,128,512]{2,1,0:T(8,128)S(1)} %get-tuple-element.207, ...), kind=kLoop, calls=%fused_computation.10.clone.1 | loop fusion | flops 1572864 | bytes 8126464 | tf_op jit(solution)/shard_map/while/body/eval_jaxpr/reduce_sum | solution.py:41
  94.1 2.2 %bitcast_dynamic-update-slice_fusion.2 = (f32[12,128,512]{2,1,0:T(8,128)}, f32[128,512]{1,0:T(8,128)}, f32[1,128,512]{2,1,0:T(8,128)S(1)}) fusion(f32[12,128,512]{2,1,0:T(8,128)} %get-tuple-element.227, s32[]{:T(128)} %get-tuple-element.224, f32[6,128,512]{2,1,0:T(8,128)S(1)} %get-tuple-element.208, f32[1,128,512]{2,1,0:T(8,128)S(1)} %copy.39, ...), kind=kLoop, calls=%fused_computation.19.clone.1 | loop fusion | flops 786432 | bytes 2361857 | tf_op jit(solution)/shard_map/while/body/jit(dynamic_update_index_in_dim)/dynamic_update_slice | solution.py:48
  98.9 2.7 %fusion.43 = (f32[128,512]{1,0:T(8,128)}, f32[5,128,512]{2,1,0:T(8,128)}) fusion(f32[6,128,512]{2,1,0:T(8,128)S(1)} %get-tuple-element.205, f32[6,128,512]{2,1,0:T(8,128)S(1)} %get-tuple-element.206, f32[6,128,512]{2,1,0:T(8,128)S(1)} %get-tuple-element.225, f32[6,128,512]{2,1,0:T(8,128)S(1)} %get-tuple-element.207, ...), kind=kLoop, calls=%fused_computation.10.clone.1 | loop fusion | flops 1572864 | bytes 8126464 | tf_op jit(solution)/shard_map/while/body/eval_jaxpr/reduce_sum | solution.py:41
  101.6 2.3 %bitcast_dynamic-update-slice_fusion.2 = (f32[12,128,512]{2,1,0:T(8,128)}, f32[128,512]{1,0:T(8,128)}, f32[1,128,512]{2,1,0:T(8,128)S(1)}) fusion(f32[12,128,512]{2,1,0:T(8,128)} %get-tuple-element.227, s32[]{:T(128)} %get-tuple-element.224, f32[6,128,512]{2,1,0:T(8,128)S(1)} %get-tuple-element.208, f32[1,128,512]{2,1,0:T(8,128)S(1)} %copy.39, ...), kind=kLoop, calls=%fused_computation.19.clone.1 | loop fusion | flops 786432 | bytes 2361857 | tf_op jit(solution)/shard_map/while/body/jit(dynamic_update_index_in_dim)/dynamic_update_slice | solution.py:48
  106.4 2.7 %fusion.43 = (f32[128,512]{1,0:T(8,128)}, f32[5,128,512]{2,1,0:T(8,128)}) fusion(f32[6,128,512]{2,1,0:T(8,128)S(1)} %get-tuple-element.205, f32[6,128,512]{2,1,0:T(8,128)S(1)} %get-tuple-element.206, f32[6,128,512]{2,1,0:T(8,128)S(1)} %get-tuple-element.225, f32[6,128,512]{2,1,0:T(8,128)S(1)} %get-tuple-element.207, ...), kind=kLoop, calls=%fused_computation.10.clone.1 | loop fusion | flops 1572864 | bytes 8126464 | tf_op jit(solution)/shard_map/while/body/eval_jaxpr/reduce_sum | solution.py:41
  109.2 2.2 %bitcast_dynamic-update-slice_fusion.2 = (f32[12,128,512]{2,1,0:T(8,128)}, f32[128,512]{1,0:T(8,128)}, f32[1,128,512]{2,1,0:T(8,128)S(1)}) fusion(f32[12,128,512]{2,1,0:T(8,128)} %get-tuple-element.227, s32[]{:T(128)} %get-tuple-element.224, f32[6,128,512]{2,1,0:T(8,128)S(1)} %get-tuple-element.208, f32[1,128,512]{2,1,0:T(8,128)S(1)} %copy.39, ...), kind=kLoop, calls=%fused_computation.19.clone.1 | loop fusion | flops 786432 | bytes 2361857 | tf_op jit(solution)/shard_map/while/body/jit(dynamic_update_index_in_dim)/dynamic_update_slice | solution.py:48
  113.9 2.7 %fusion.43 = (f32[128,512]{1,0:T(8,128)}, f32[5,128,512]{2,1,0:T(8,128)}) fusion(f32[6,128,512]{2,1,0:T(8,128)S(1)} %get-tuple-element.205, f32[6,128,512]{2,1,0:T(8,128)S(1)} %get-tuple-element.206, f32[6,128,512]{2,1,0:T(8,128)S(1)} %get-tuple-element.225, f32[6,128,512]{2,1,0:T(8,128)S(1)} %get-tuple-element.207, ...), kind=kLoop, calls=%fused_computation.10.clone.1 | loop fusion | flops 1572864 | bytes 8126464 | tf_op jit(solution)/shard_map/while/body/eval_jaxpr/reduce_sum | solution.py:41
  116.7 2.2 %bitcast_dynamic-update-slice_fusion.2 = (f32[12,128,512]{2,1,0:T(8,128)}, f32[128,512]{1,0:T(8,128)}, f32[1,128,512]{2,1,0:T(8,128)S(1)}) fusion(f32[12,128,512]{2,1,0:T(8,128)} %get-tuple-element.227, s32[]{:T(128)} %get-tuple-element.224, f32[6,128,512]{2,1,0:T(8,128)S(1)} %get-tuple-element.208, f32[1,128,512]{2,1,0:T(8,128)S(1)} %copy.39, ...), kind=kLoop, calls=%fused_computation.19.clone.1 | loop fusion | flops 786432 | bytes 2361857 | tf_op jit(solution)/shard_map/while/body/jit(dynamic_update_index_in_dim)/dynamic_update_slice | solution.py:48
  121.4 2.7 %fusion.43 = (f32[128,512]{1,0:T(8,128)}, f32[5,128,512]{2,1,0:T(8,128)}) fusion(f32[6,128,512]{2,1,0:T(8,128)S(1)} %get-tuple-element.205, f32[6,128,512]{2,1,0:T(8,128)S(1)} %get-tuple-element.206, f32[6,128,512]{2,1,0:T(8,128)S(1)} %get-tuple-element.225, f32[6,128,512]{2,1,0:T(8,128)S(1)} %get-tuple-element.207, ...), kind=kLoop, calls=%fused_computation.10.clone.1 | loop fusion | flops 1572864 | bytes 8126464 | tf_op jit(solution)/shard_map/while/body/eval_jaxpr/reduce_sum | solution.py:41
  124.2 2.2 %bitcast_dynamic-update-slice_fusion.2 = (f32[12,128,512]{2,1,0:T(8,128)}, f32[128,512]{1,0:T(8,128)}, f32[1,128,512]{2,1,0:T(8,128)S(1)}) fusion(f32[12,128,512]{2,1,0:T(8,128)} %get-tuple-element.227, s32[]{:T(128)} %get-tuple-element.224, f32[6,128,512]{2,1,0:T(8,128)S(1)} %get-tuple-element.208, f32[1,128,512]{2,1,0:T(8,128)S(1)} %copy.39, ...), kind=kLoop, calls=%fused_computation.19.clone.1 | loop fusion | flops 786432 | bytes 2361857 | tf_op jit(solution)/shard_map/while/body/jit(dynamic_update_index_in_dim)/dynamic_update_slice | solution.py:48
  128.9 2.7 %fusion.43 = (f32[128,512]{1,0:T(8,128)}, f32[5,128,512]{2,1,0:T(8,128)}) fusion(f32[6,128,512]{2,1,0:T(8,128)S(1)} %get-tuple-element.205, f32[6,128,512]{2,1,0:T(8,128)S(1)} %get-tuple-element.206, f32[6,128,512]{2,1,0:T(8,128)S(1)} %get-tuple-element.225, f32[6,128,512]{2,1,0:T(8,128)S(1)} %get-tuple-element.207, ...), kind=kLoop, calls=%fused_computation.10.clone.1 | loop fusion | flops 1572864 | bytes 8126464 | tf_op jit(solution)/shard_map/while/body/eval_jaxpr/reduce_sum | solution.py:41
  131.6 2.2 %bitcast_dynamic-update-slice_fusion.2 = (f32[12,128,512]{2,1,0:T(8,128)}, f32[128,512]{1,0:T(8,128)}, f32[1,128,512]{2,1,0:T(8,128)S(1)}) fusion(f32[12,128,512]{2,1,0:T(8,128)} %get-tuple-element.227, s32[]{:T(128)} %get-tuple-element.224, f32[6,128,512]{2,1,0:T(8,128)S(1)} %get-tuple-element.208, f32[1,128,512]{2,1,0:T(8,128)S(1)} %copy.39, ...), kind=kLoop, calls=%fused_computation.19.clone.1 | loop fusion | flops 786432 | bytes 2361857 | tf_op jit(solution)/shard_map/while/body/jit(dynamic_update_index_in_dim)/dynamic_update_slice | solution.py:48
  137.0 3.4 %all-to-all-start.1 = ((f32[8,8,384]{2,1,0:T(8,128)}), f32[8,8,384]{2,1,0:T(8,128)S(1)}, u32[]{:S(2)}, u32[]{:S(2)}) async-start(f32[8,8,384]{2,1,0:T(8,128)} %bitcast.5), calls=%async_computation.1 | async-start | bytes 196608 | tf_op jit(solution)/shard_map/all_to_all | solution.py:123
  140.6 4.9 %all-to-all-done.1 = f32[8,8,384]{2,1,0:T(8,128)S(1)} async-done(((f32[8,8,384]{2,1,0:T(8,128)}), f32[8,8,384]{2,1,0:T(8,128)S(1)}, u32[]{:S(2)}, u32[]{:S(2)}) %all-to-all-start.1) | async-done | bytes 98336 | tf_op jit(solution)/shard_map/all_to_all | solution.py:123
  146.8 13.2 %all-gather = f32[24,3,64]{2,1,0:T(4,128)S(1)} all-gather(f32[6,3,64]{2,1,0:T(4,128)S(1)} %copy.29), channel_id=2, replica_groups=mesh['loan'=8,'path'=4] {'path'}, dimensions={0}, use_global_device_ids=true | all-gather | bytes 23040 | tf_op jit(solution)/shard_map/all_gather | solution.py:11
  (185 shorter events, 51.6 us)
Async XLA Ops:
  7.2 14.3 %copy-start.9 = (s32[2,32]{1,0:T(2,128)S(1)}, s32[2,32]{1,0:T(2,128)}, u32[]{:S(2)}) copy-start(s32[2,32]{1,0:T(2,128)} %param.14) | copy-start | bytes 772
  7.2 14.3 %copy-start.5 = (s32[64,6]{0,1:T(8,128)S(1)}, s32[64,6]{0,1:T(8,128)}, u32[]{:S(2)}) copy-start(s32[64,6]{0,1:T(8,128)} %param.23) | copy-start | bytes 4612
  7.2 14.4 %copy-start.7 = (s32[512]{0:T(512)S(1)}, s32[512]{0:T(512)}, u32[]{:S(2)}) copy-start(s32[512]{0:T(512)} %param.15) | copy-start | bytes 6148
  7.2 14.6 %copy-start.6 = (s32[512]{0:T(512)S(1)}, s32[512]{0:T(512)}, u32[]{:S(2)}) copy-start(s32[512]{0:T(512)} %param.18) | copy-start | bytes 6148
  7.2 14.6 %copy-start.8 = (f32[512]{0:T(512)S(1)}, f32[512]{0:T(512)}, u32[]{:S(2)}) copy-start(f32[512]{0:T(512)} %param.20) | copy-start | bytes 6148
  7.2 31.6 %all-gather.3.cloned.1.call-start = ((), (), s32[]{:S(2)}) async-start(), calls=%async_computation.3 | async-start | bytes 1916928 | tf_op jit(solution)/shard_map/all_gather | solution.py:78
  13.2 9.8 %all-to-all-start = ((f32[8,8,1]{1,2,0:T(1,128)}), f32[8,8,1]{1,2,0:T(1,128)S(1)}, u32[]{:S(2)}, u32[]{:S(2)}) async-start(f32[8,8,1]{1,2,0:T(1,128)} %bitcast), calls=%async_computation | async-start | bytes 8192 | tf_op jit(solution)/shard_map/all_to_all | solution.py:125
  23.0 7.9 %all-to-all-start.2 = ((f32[8,8,1]{1,2,0:T(1,128)}), f32[8,8,1]{1,2,0:T(1,128)S(1)}, u32[]{:S(2)}, u32[]{:S(2)}) async-start(f32[8,8,1]{1,2,0:T(1,128)} %bitcast.10), calls=%async_computation.2 | async-start | bytes 8192 | tf_op jit(solution)/shard_map/all_to_all | solution.py:124
  46.4 2.8 %copy-start = (f32[6,128,512]{2,1,0:T(8,128)}, f32[6,128,512]{2,1,0:T(8,128)S(1)}, u32[]{:S(2)}) copy-start(f32[6,128,512]{2,1,0:T(8,128)S(1)} %get-tuple-element.207) | copy-start | bytes 4718596 | tf_op jit(solution)/shard_map/while
  53.9 2.8 %copy-start = (f32[6,128,512]{2,1,0:T(8,128)}, f32[6,128,512]{2,1,0:T(8,128)S(1)}, u32[]{:S(2)}) copy-start(f32[6,128,512]{2,1,0:T(8,128)S(1)} %get-tuple-element.207) | copy-start | bytes 4718596 | tf_op jit(solution)/shard_map/while
  56.6 2.2 %copy-start.1 = (f32[5,128,512]{2,1,0:T(8,128)S(1)}, f32[5,128,512]{2,1,0:T(8,128)}, u32[]{:S(2)}) copy-start(f32[5,128,512]{2,1,0:T(8,128)} %get-tuple-element.209) | copy-start | bytes 3932164 | tf_op jit(solution)/shard_map/while
  61.4 2.8 %copy-start = (f32[6,128,512]{2,1,0:T(8,128)}, f32[6,128,512]{2,1,0:T(8,128)S(1)}, u32[]{:S(2)}) copy-start(f32[6,128,512]{2,1,0:T(8,128)S(1)} %get-tuple-element.207) | copy-start | bytes 4718596 | tf_op jit(solution)/shard_map/while
  64.1 2.2 %copy-start.1 = (f32[5,128,512]{2,1,0:T(8,128)S(1)}, f32[5,128,512]{2,1,0:T(8,128)}, u32[]{:S(2)}) copy-start(f32[5,128,512]{2,1,0:T(8,128)} %get-tuple-element.209) | copy-start | bytes 3932164 | tf_op jit(solution)/shard_map/while
  68.9 2.8 %copy-start = (f32[6,128,512]{2,1,0:T(8,128)}, f32[6,128,512]{2,1,0:T(8,128)S(1)}, u32[]{:S(2)}) copy-start(f32[6,128,512]{2,1,0:T(8,128)S(1)} %get-tuple-element.207) | copy-start | bytes 4718596 | tf_op jit(solution)/shard_map/while
  71.7 2.2 %copy-start.1 = (f32[5,128,512]{2,1,0:T(8,128)S(1)}, f32[5,128,512]{2,1,0:T(8,128)}, u32[]{:S(2)}) copy-start(f32[5,128,512]{2,1,0:T(8,128)} %get-tuple-element.209) | copy-start | bytes 3932164 | tf_op jit(solution)/shard_map/while
  76.4 2.8 %copy-start = (f32[6,128,512]{2,1,0:T(8,128)}, f32[6,128,512]{2,1,0:T(8,128)S(1)}, u32[]{:S(2)}) copy-start(f32[6,128,512]{2,1,0:T(8,128)S(1)} %get-tuple-element.207) | copy-start | bytes 4718596 | tf_op jit(solution)/shard_map/while
  79.1 2.2 %copy-start.1 = (f32[5,128,512]{2,1,0:T(8,128)S(1)}, f32[5,128,512]{2,1,0:T(8,128)}, u32[]{:S(2)}) copy-start(f32[5,128,512]{2,1,0:T(8,128)} %get-tuple-element.209) | copy-start | bytes 3932164 | tf_op jit(solution)/shard_map/while
  83.9 2.8 %copy-start = (f32[6,128,512]{2,1,0:T(8,128)}, f32[6,128,512]{2,1,0:T(8,128)S(1)}, u32[]{:S(2)}) copy-start(f32[6,128,512]{2,1,0:T(8,128)S(1)} %get-tuple-element.207) | copy-start | bytes 4718596 | tf_op jit(solution)/shard_map/while
  86.7 2.2 %copy-start.1 = (f32[5,128,512]{2,1,0:T(8,128)S(1)}, f32[5,128,512]{2,1,0:T(8,128)}, u32[]{:S(2)}) copy-start(f32[5,128,512]{2,1,0:T(8,128)} %get-tuple-element.209) | copy-start | bytes 3932164 | tf_op jit(solution)/shard_map/while
  91.4 2.8 %copy-start = (f32[6,128,512]{2,1,0:T(8,128)}, f32[6,128,512]{2,1,0:T(8,128)S(1)}, u32[]{:S(2)}) copy-start(f32[6,128,512]{2,1,0:T(8,128)S(1)} %get-tuple-element.207) | copy-start | bytes 4718596 | tf_op jit(solution)/shard_map/while
  94.1 2.2 %copy-start.1 = (f32[5,128,512]{2,1,0:T(8,128)S(1)}, f32[5,128,512]{2,1,0:T(8,128)}, u32[]{:S(2)}) copy-start(f32[5,128,512]{2,1,0:T(8,128)} %get-tuple-element.209) | copy-start | bytes 3932164 | tf_op jit(solution)/shard_map/while
  98.9 2.8 %copy-start = (f32[6,128,512]{2,1,0:T(8,128)}, f32[6,128,512]{2,1,0:T(8,128)S(1)}, u32[]{:S(2)}) copy-start(f32[6,128,512]{2,1,0:T(8,128)S(1)} %get-tuple-element.207) | copy-start | bytes 4718596 | tf_op jit(solution)/shard_map/while
  101.6 2.3 %copy-start.1 = (f32[5,128,512]{2,1,0:T(8,128)S(1)}, f32[5,128,512]{2,1,0:T(8,128)}, u32[]{:S(2)}) copy-start(f32[5,128,512]{2,1,0:T(8,128)} %get-tuple-element.209) | copy-start | bytes 3932164 | tf_op jit(solution)/shard_map/while
  106.4 2.8 %copy-start = (f32[6,128,512]{2,1,0:T(8,128)}, f32[6,128,512]{2,1,0:T(8,128)S(1)}, u32[]{:S(2)}) copy-start(f32[6,128,512]{2,1,0:T(8,128)S(1)} %get-tuple-element.207) | copy-start | bytes 4718596 | tf_op jit(solution)/shard_map/while
  109.2 2.2 %copy-start.1 = (f32[5,128,512]{2,1,0:T(8,128)S(1)}, f32[5,128,512]{2,1,0:T(8,128)}, u32[]{:S(2)}) copy-start(f32[5,128,512]{2,1,0:T(8,128)} %get-tuple-element.209) | copy-start | bytes 3932164 | tf_op jit(solution)/shard_map/while
  113.9 2.8 %copy-start = (f32[6,128,512]{2,1,0:T(8,128)}, f32[6,128,512]{2,1,0:T(8,128)S(1)}, u32[]{:S(2)}) copy-start(f32[6,128,512]{2,1,0:T(8,128)S(1)} %get-tuple-element.207) | copy-start | bytes 4718596 | tf_op jit(solution)/shard_map/while
  116.7 2.2 %copy-start.1 = (f32[5,128,512]{2,1,0:T(8,128)S(1)}, f32[5,128,512]{2,1,0:T(8,128)}, u32[]{:S(2)}) copy-start(f32[5,128,512]{2,1,0:T(8,128)} %get-tuple-element.209) | copy-start | bytes 3932164 | tf_op jit(solution)/shard_map/while
  121.4 2.8 %copy-start = (f32[6,128,512]{2,1,0:T(8,128)}, f32[6,128,512]{2,1,0:T(8,128)S(1)}, u32[]{:S(2)}) copy-start(f32[6,128,512]{2,1,0:T(8,128)S(1)} %get-tuple-element.207) | copy-start | bytes 4718596 | tf_op jit(solution)/shard_map/while
  124.2 2.2 %copy-start.1 = (f32[5,128,512]{2,1,0:T(8,128)S(1)}, f32[5,128,512]{2,1,0:T(8,128)}, u32[]{:S(2)}) copy-start(f32[5,128,512]{2,1,0:T(8,128)} %get-tuple-element.209) | copy-start | bytes 3932164 | tf_op jit(solution)/shard_map/while
  128.9 2.8 %copy-start = (f32[6,128,512]{2,1,0:T(8,128)}, f32[6,128,512]{2,1,0:T(8,128)S(1)}, u32[]{:S(2)}) copy-start(f32[6,128,512]{2,1,0:T(8,128)S(1)} %get-tuple-element.207) | copy-start | bytes 4718596 | tf_op jit(solution)/shard_map/while
  131.6 2.2 %copy-start.1 = (f32[5,128,512]{2,1,0:T(8,128)S(1)}, f32[5,128,512]{2,1,0:T(8,128)}, u32[]{:S(2)}) copy-start(f32[5,128,512]{2,1,0:T(8,128)} %get-tuple-element.209) | copy-start | bytes 3932164 | tf_op jit(solution)/shard_map/while
  137.0 8.5 %all-to-all-start.1 = ((f32[8,8,384]{2,1,0:T(8,128)}), f32[8,8,384]{2,1,0:T(8,128)S(1)}, u32[]{:S(2)}, u32[]{:S(2)}) async-start(f32[8,8,384]{2,1,0:T(8,128)} %bitcast.5), calls=%async_computation.1 | async-start | bytes 196608 | tf_op jit(solution)/shard_map/all_to_all | solution.py:123
  (4 other events, 4.2 us)
Sparse Core Ops, SparseCore 0:
  9.9 28.8 all-gather.2
